TPU v7x, 32 devices: a whole 2x2x4 slice. The times are simulated.
32 devices in a mesh: dp: 8 (over z, x), head: 4 (over y, core).
Axes of the slice: x: 2, y: 2, z: 4, core: 2. Of those that a mesh axis runs over, the one named last changes fastest.
Arguments:
- layer_in: bfloat16 [24576, 768], P(('dp', 'head')), may hold values from -6 to 6
- doc_ids: int32 [24576], P('dp'), may hold values from -1 to 16, as said below
- g_attn: bfloat16 [768], replicated, may hold values from 0.5 to 1.5
- w_qkv: bfloat16 [3, 768, 768], P(None, None, 'head'), may hold values from -0.21875 to 0.21875
- g_inner: bfloat16 [768], P('head'), may hold values from 0.5 to 1.5
- w_o: bfloat16 [768, 768], P('head'), may hold values from -0.21875 to 0.21875
- g_ffn: bfloat16 [768], replicated, may hold values from 0.5 to 1.5
- w_in: bfloat16 [3072, 768], P(('dp', 'head')), may hold values from -0.21875 to 0.21875
- g_hidden: bfloat16 [3072], P(('dp', 'head')), may hold values from 0.5 to 1.5
- w_out: bfloat16 [3072, 768], P(('dp', 'head')), may hold values from -0.109375 to 0.109375
- cotangent: bfloat16 [24576, 768], P(('dp', 'head')), may hold values from -6 to 6
Outputs:
- layer_out: bfloat16 [24576, 768], P(('dp', 'head'))
- grad_x: float32 [24576, 768], P(('dp', 'head'))
- grad_g_attn: float32 [768], replicated
- grad_w_qkv: float32 [3, 768, 768], P(None, None, 'head')
- grad_g_inner: float32 [768], P('head')
- grad_w_o: float32 [768, 768], P('head')
- grad_g_ffn: float32 [768], replicated
- grad_w_in: float32 [3072, 768], P(('dp', 'head'))
- grad_g_hidden: float32 [3072], P(('dp', 'head'))
- grad_w_out: float32 [3072, 768], P(('dp', 'head'))
Inputs may be any that keep to these rules, and one draw needn't show every extreme that they name: `doc_ids`: within each group of 3072 slots, document numbers start at 0 and never fall; padding (-1) fills the end of the group, at most a quarter of it, and some group has no padding; the first document of every group has exactly 2048 tokens and none has more; every document has a multiple of 64 tokens.
All inputs are finite; a program needn't handle non-finite values.
Results may differ from a plain program's by a relative error of at most 0.015.
Values may be sent and summed in bfloat16 or wider, within the bound.
No kernel may reach another device: no remote copies, remote signals or barrier semaphores. Data moves between devices by JAX's collectives and lax.ppermute only.
A program may use at most 192 MiB of HBM per device.

v0:
```python
import jax
import jax.numpy as jnp
from jax import lax
from jax.sharding import PartitionSpec as P

HEAD_DIM = 64


EPSILON = 1e-05
NEG_BIG = -1e30


def layer_norm(values, gain):
    average = jnp.mean(values, axis=-1, keepdims=True)
    spread = jnp.mean(values * values, axis=-1, keepdims=True) - average * average
    return (values - average) * lax.rsqrt(spread + EPSILON) * gain


def hidden_norm(pre_act, gain):
    return layer_norm(jax.nn.gelu(pre_act, approximate=False), gain)


def masked_scores(query_blk, keys, doc_ids, offset, block_len):
    logits = jnp.einsum(
        "qhd,khd->hqk", query_blk, keys, preferred_element_type=jnp.float32
    ) * HEAD_DIM ** (-0.5)
    query_ids = lax.dynamic_slice_in_dim(doc_ids, offset, block_len, 0)
    query_pos = offset + jnp.arange(block_len, dtype=jnp.int32)
    key_pos = jnp.arange(doc_ids.shape[0], dtype=jnp.int32)
    allowed = (query_ids[:, None] == doc_ids[None, :]) & (key_pos[None, :] <= query_pos[:, None])
    return jnp.where(allowed[None], logits, NEG_BIG)


def body(layer_in, doc_ids, g_attn, w_qkv, g_inner, w_o, g_ffn, w_in, g_hidden, w_out, cotangent):
    row_count = layer_in.shape[0]
    width = layer_in.shape[1]
    group_len = doc_ids.shape[0]
    local_width = w_qkv.shape[2]
    head_count = local_width // HEAD_DIM
    block_len = min(512, group_len)
    block_total = group_len // block_len
    scale = HEAD_DIM ** (-0.5)
    factor = (row_count * lax.axis_size("head") * lax.axis_size("dp")) ** (-0.5)
    own_ids = lax.dynamic_slice_in_dim(doc_ids, lax.axis_index("head") * row_count, row_count, 0)
    valid = (own_ids >= 0).astype(jnp.float32)[:, None]
    start_x = layer_in.astype(jnp.float32) * valid
    normed_f, ln_first_back = jax.vjp(layer_norm, start_x, g_attn.astype(jnp.float32))
    normed = normed_f.astype(jnp.bfloat16)
    gathered = lax.all_gather(normed, "head", axis=0, tiled=True)
    proj_qkv = jnp.einsum(
        "td,cde->cte", gathered, w_qkv, preferred_element_type=jnp.float32
    ).astype(jnp.bfloat16)
    queries = proj_qkv[0].reshape(group_len, head_count, HEAD_DIM)
    keys = proj_qkv[1].reshape(group_len, head_count, HEAD_DIM)
    values = proj_qkv[2].reshape(group_len, head_count, HEAD_DIM)

    def forward_block(block_idx):
        offset = block_idx * block_len
        query_blk = lax.dynamic_slice_in_dim(queries, offset, block_len, 0)
        logits = masked_scores(query_blk, keys, doc_ids, offset, block_len)
        row_max = jnp.max(logits, axis=-1, keepdims=True)
        expo = jnp.exp(logits - row_max)
        row_total = jnp.sum(expo, axis=-1, keepdims=True)
        probs = expo / row_total
        block_out = jnp.einsum(
            "hqk,khd->qhd", probs.astype(jnp.bfloat16), values, preferred_element_type=jnp.float32
        )
        return (block_out, (row_max + jnp.log(row_total))[:, :, 0])

    block_ids = jnp.arange(block_total, dtype=jnp.int32)
    outputs, log_sums = lax.map(forward_block, block_ids)
    attended = outputs.reshape(group_len, local_width)
    part_sum = jnp.sum(attended, axis=-1)
    part_square = jnp.sum(attended * attended, axis=-1)
    total_sum, total_square = lax.psum((part_sum, part_square), "head")
    average = (total_sum / width)[:, None]
    rstd = lax.rsqrt((total_square / width)[:, None] - average * average + EPSILON)
    centered = (attended - average) * rstd
    gain_inner = g_inner.astype(jnp.float32)
    normed_out = (centered * gain_inner).astype(jnp.bfloat16)
    mixed = lax.psum_scatter(
        jnp.dot(normed_out, w_o, preferred_element_type=jnp.float32),
        "head",
        scatter_dimension=0,
        tiled=True,
    )
    residual = start_x + mixed
    win_full, wout_full, ghid_full = (
        lax.all_gather(w_in, ("dp", "head"), axis=0, tiled=True),
        lax.all_gather(w_out, ("dp", "head"), axis=0, tiled=True),
        lax.all_gather(g_hidden, ("dp", "head"), axis=0, tiled=True),
    )
    ffn_in_f, ln_ffn_back = jax.vjp(layer_norm, residual, g_ffn.astype(jnp.float32))
    ffn_input = ffn_in_f.astype(jnp.bfloat16)
    pre_act = lax.dot_general(
        ffn_input, win_full, (((1,), (1,)), ((), ())), preferred_element_type=jnp.float32
    )
    post_f, hidden_back = jax.vjp(hidden_norm, pre_act, ghid_full.astype(jnp.float32))
    post_norm = post_f.astype(jnp.bfloat16)
    ffn_out = jnp.dot(post_norm, wout_full, preferred_element_type=jnp.float32)
    result = (residual + ffn_out).astype(jnp.bfloat16)
    grad_y = cotangent.astype(jnp.float32)
    win_back, wout_back = (
        lax.all_gather(w_in, ("dp", "head"), axis=0, tiled=True),
        lax.all_gather(w_out, ("dp", "head"), axis=0, tiled=True),
    )
    grad_low = grad_y.astype(jnp.bfloat16)
    grad_wout = lax.dot_general(
        post_norm, grad_low, (((0,), (0,)), ((), ())), preferred_element_type=jnp.float32
    )
    grad_post = lax.dot_general(
        grad_low, wout_back, (((1,), (1,)), ((), ())), preferred_element_type=jnp.float32
    )
    grad_pre, grad_ghid = hidden_back(grad_post)
    grad_pre_low = grad_pre.astype(jnp.bfloat16)
    grad_win = lax.dot_general(
        grad_pre_low, ffn_input, (((0,), (0,)), ((), ())), preferred_element_type=jnp.float32
    )
    grad_ffn_in = jnp.dot(grad_pre_low, win_back, preferred_element_type=jnp.float32)
    grad_res_ln, grad_gffn = ln_ffn_back(grad_ffn_in)
    grad_res = grad_y + grad_res_ln
    sum_win, sum_wout, sum_ghid = (
        lax.psum_scatter(grad_win, ("dp", "head"), scatter_dimension=0, tiled=True),
        lax.psum_scatter(grad_wout, ("dp", "head"), scatter_dimension=0, tiled=True),
        lax.psum_scatter(grad_ghid, ("dp", "head"), scatter_dimension=0, tiled=True),
    )
    grad_mixed = lax.all_gather(grad_res.astype(jnp.bfloat16), "head", axis=0, tiled=True)
    grad_wo = lax.dot_general(
        normed_out, grad_mixed, (((0,), (0,)), ((), ())), preferred_element_type=jnp.float32
    )
    grad_normed_out = lax.dot_general(
        grad_mixed, w_o, (((1,), (1,)), ((), ())), preferred_element_type=jnp.float32
    )
    grad_ginner = jnp.sum(grad_normed_out * centered, axis=0)
    grad_hat = grad_normed_out * gain_inner
    part_first = jnp.sum(grad_hat, axis=-1)
    part_second = jnp.sum(grad_hat * centered, axis=-1)
    total_first, total_second = lax.psum((part_first, part_second), "head")
    grad_attended = rstd * (
        grad_hat - (total_first / width)[:, None] - centered * (total_second / width)[:, None]
    )
    grad_out = grad_attended.astype(jnp.bfloat16).reshape(group_len, head_count, HEAD_DIM)

    def backward_block(carry, block_idx):
        grad_keys, grad_values = carry
        offset = block_idx * block_len
        query_blk = lax.dynamic_slice_in_dim(queries, offset, block_len, 0)
        grad_blk = lax.dynamic_slice_in_dim(grad_out, offset, block_len, 0)
        logits = masked_scores(query_blk, keys, doc_ids, offset, block_len)
        probs = jnp.exp(logits - log_sums[block_idx][:, :, None])
        grad_values = grad_values + jnp.einsum(
            "hqk,qhd->khd", probs.astype(jnp.bfloat16), grad_blk, preferred_element_type=jnp.float32
        )
        grad_probs = jnp.einsum(
            "qhd,khd->hqk", grad_blk, values, preferred_element_type=jnp.float32
        )
        inner = jnp.sum(probs * grad_probs, axis=-1, keepdims=True)
        grad_logits = (probs * (grad_probs - inner)).astype(jnp.bfloat16)
        grad_query = (
            jnp.einsum("hqk,khd->qhd", grad_logits, keys, preferred_element_type=jnp.float32)
            * scale
        )
        grad_keys = (
            grad_keys
            + jnp.einsum("hqk,qhd->khd", grad_logits, query_blk, preferred_element_type=jnp.float32)
            * scale
        )
        return ((grad_keys, grad_values), grad_query)

    zeros_kv = jnp.zeros((group_len, head_count, HEAD_DIM), jnp.float32)
    carried, grad_queries = lax.scan(backward_block, (zeros_kv, zeros_kv), block_ids)
    grad_qkv = jnp.stack(
        [
            grad_queries.reshape(group_len, local_width),
            carried[0].reshape(group_len, local_width),
            carried[1].reshape(group_len, local_width),
        ]
    ).astype(jnp.bfloat16)
    grad_wqkv = jnp.einsum("td,cte->cde", gathered, grad_qkv, preferred_element_type=jnp.float32)
    grad_normed = lax.psum_scatter(
        jnp.einsum("cte,cde->td", grad_qkv, w_qkv, preferred_element_type=jnp.float32).astype(
            jnp.bfloat16
        ),
        "head",
        scatter_dimension=0,
        tiled=True,
    ).astype(jnp.float32)
    grad_x_ln, grad_gattn = ln_first_back(grad_normed)
    grad_input = (grad_res + grad_x_ln) * valid
    sum_wqkv, sum_wo, sum_ginner = lax.psum((grad_wqkv, grad_wo, grad_ginner), "dp")
    sum_gattn, sum_gffn = lax.psum((grad_gattn, grad_gffn), ("dp", "head"))
    return (
        result,
        grad_input,
        sum_gattn * factor,
        sum_wqkv * factor,
        sum_ginner * factor,
        sum_wo * factor,
        sum_gffn * factor,
        sum_win * factor,
        sum_ghid * factor,
        sum_wout * factor,
    )


def solution(mesh):
    placed = (
        P(("dp", "head"), None),
        P("dp"),
        P(),
        P(None, None, "head"),
        P("head"),
        P("head", None),
        P(),
        P(("dp", "head"), None),
        P(("dp", "head")),
        P(("dp", "head"), None),
        P(("dp", "head"), None),
    )
    return jax.shard_map(
        body,
        mesh=mesh,
        in_specs=placed,
        out_specs=(
            P(("dp", "head"), None),
            P(("dp", "head"), None),
            P(),
            P(None, None, "head"),
            P("head"),
            P("head", None),
            P(),
            P(("dp", "head"), None),
            P(("dp", "head")),
            P(("dp", "head"), None),
        ),
        check_vma=False,
    )
```

profile of v0, /device:TPU:0, one launch (start us, length us, event | category | flops | bytes accessed | tf_op | source)
XLA Modules:
  0.0 1430.1 jit_solution(1142854543343633926)
XLA Ops:
  16.2 39.7 %all-gather.5.cloned.1.call-done = bf16[3072,768]{1,0:T(8,128)(2,1)} async-done(((bf16[768,768]{1,0:T(8,128)(2,1)}), bf16[3072,768]{1,0:T(8,128)(2,1)}) %all-gather.5.cloned.1.call-update) | async-done | bytes 4718608 | tf_op jit(solution)/shard_map/all_gather | solution.py:49
  62.9 139.7 %while.29 = (s32[]{:T(128)}, f32[6,512,3,64]{1,3,2,0:T(8,128)}, f32[6,3,512]{2,1,0:T(4,128)}, s32[6]{0:T(128)S(1)}, s32[3072]{0:T(1024)S(1)}, /*index=5*/bf16[30...) while((s32[]{:T(128)}, f32[6,512,3,64]{1,3,2,0:T(8,128)}, ...), condition=%wide.region_5.6_spmd.clone, body=%wide.region_2.5_spmd.sunk.clone | while | flops 1269300224 | bytes 72230080 | solution.py:71
  212.4 10.3 all-reduce.5
  230.5 42.0 %all-reduce = bf16[3072]{0:T(1024)(128)(2,1)S(1)} all-reduce(bf16[3072]{0:T(1024)(128)(2,1)S(1)} %dynamic-update-slice), channel_id=1, replica_groups=mesh['dp'=8,'head'=4] {'dp','head'}, use_global_device_ids=true, to_apply=%add | all-reduce | flops 3072 | bytes 12288
  272.5 38.7 %reduce-scatter.5.cloned.1.call-done = f32[768,768]{1,0:T(8,128)} async-done(((f32[3072,768]{1,0:T(8,128)}), f32[768,768]{1,0:T(8,128)}) %reduce-scatter.5.cloned.1.call-update) | async-done | bytes 2359312 | tf_op jit(solution)/shard_map/reduce_scatter | solution.py:81
  315.1 11.8 all-gather.7.cloned.1.call-done
  326.9 29.3 %fusion.77 = (f32[768]{0:T(1024)S(1)}, f32[768]{0:T(1024)S(1)}, f32[768,3072]{1,0:T(8,128)}, f32[768,3072]{1,0:T(8,128)}, f32[768,3072]{1,0:T(8,128)}) fusion(bf16[3072,768]{1,0:T(8,128)(2,1)} %all-gather.7.cloned.1.call-done, f32[768,768]{1,0:T(8,128)} %get-tuple-element.224, f32[768]{0:T(1024)S(1)} %convert_element_type.76, ...), kind=kOutput, calls=%fused_computation.152 | convolution fusion | flops 3784309248 | bytes 35404800 | tf_op jit(solution)/shard_map/dot_general | solution.py:95
  356.2 35.3 %all-gather.9.cloned.1.call-done = bf16[3072,768]{1,0:T(8,128)(2,1)} async-done(((bf16[96,768]{1,0:T(8,128)(2,1)}), bf16[3072,768]{1,0:T(8,128)(2,1)}) %all-gather.9.cloned.1.call-update) | async-done | bytes 4718608 | tf_op jit(solution)/shard_map/all_gather | solution.py:90
  391.5 12.9 multiply_reduce_fusion.1
  404.5 12.7 add_convert_fusion
  417.2 9.0 multiply_reduce_fusion.5
  430.1 34.7 %all-gather.11.cloned.1.call-done = bf16[3072,768]{1,0:T(8,128)(2,1)} async-done(((bf16[768,768]{1,0:T(8,128)(2,1)}), bf16[3072,768]{1,0:T(8,128)(2,1)}) %all-gather.11.cloned.1.call-update) | async-done | bytes 4718608 | tf_op jit(solution)/shard_map/all_gather | solution.py:127
  470.8 10.3 all-reduce.4
  484.5 430.1 %while.30 = (s32[]{:T(128)}, f32[3072,3,64]{0,2,1:T(8,128)}, f32[3072,3,64]{0,2,1:T(8,128)}, bf16[6,512,3,64]{1,3,2,0:T(8,128)(2,1)}, s32[6]{0:T(128)S(1)}, /*in...) while((s32[]{:T(128)}, f32[3072,3,64]{0,2,1:T(8,128)}, ...), condition=%wide.region_25.26_spmd.clone.clone, body=%wide.region_23.25_spmd.clone.sunk.clone | while | flops 3098442752 | bytes 199820048 | solution.py:171
  487.9 10.5 fusion.166
  500.8 14.3 multiply_reduce_fusion.16
  515.1 17.8 %multiply_convert_fusion.12 = bf16[3,512,3072]{2,1,0:T(8,128)(2,1)} fusion(f32[3,512,3072]{2,1,0:T(8,128)} %get-tuple-element.414, f32[3,512,3072]{2,1,0:T(8,128)} %fusion.166, f32[3,512]{1,0:T(4,128)S(1)} %get-tuple-element.415, f32[3,512]{1,0:T(4,128)S(1)} %dynamic-slice_bitcast_fusion.3, pred[512,3072]{1,0:T(8,128)(4,1)S(1)} %fusion.167), kind=kLoop, calls=%fused_computation.17.clone.1.clone | loop fusion | flops 28311552 | bytes 48771072 | tf_op jit(solution)/shard_map/while/body/eval_jaxpr/convert_element_type | solution.py:158
  545.0 10.2 fusion.169
  558.5 10.5 fusion.166
  571.4 14.3 multiply_reduce_fusion.16
  585.7 17.8 %multiply_convert_fusion.12 = bf16[3,512,3072]{2,1,0:T(8,128)(2,1)} fusion(f32[3,512,3072]{2,1,0:T(8,128)} %get-tuple-element.414, f32[3,512,3072]{2,1,0:T(8,128)} %fusion.166, f32[3,512]{1,0:T(4,128)S(1)} %get-tuple-element.415, f32[3,512]{1,0:T(4,128)S(1)} %dynamic-slice_bitcast_fusion.3, pred[512,3072]{1,0:T(8,128)(4,1)S(1)} %fusion.167), kind=kLoop, calls=%fused_computation.17.clone.1.clone | loop fusion | flops 28311552 | bytes 48771072 | tf_op jit(solution)/shard_map/while/body/eval_jaxpr/convert_element_type | solution.py:158
  616.2 10.8 fusion.169
  630.3 10.5 fusion.166
  643.2 14.3 multiply_reduce_fusion.16
  657.5 17.8 %multiply_convert_fusion.12 = bf16[3,512,3072]{2,1,0:T(8,128)(2,1)} fusion(f32[3,512,3072]{2,1,0:T(8,128)} %get-tuple-element.414, f32[3,512,3072]{2,1,0:T(8,128)} %fusion.166, f32[3,512]{1,0:T(4,128)S(1)} %get-tuple-element.415, f32[3,512]{1,0:T(4,128)S(1)} %dynamic-slice_bitcast_fusion.3, pred[512,3072]{1,0:T(8,128)(4,1)S(1)} %fusion.167), kind=kLoop, calls=%fused_computation.17.clone.1.clone | loop fusion | flops 28311552 | bytes 48771072 | tf_op jit(solution)/shard_map/while/body/eval_jaxpr/convert_element_type | solution.py:158
  688.0 10.8 fusion.169
  702.1 10.5 fusion.166
  715.1 14.3 multiply_reduce_fusion.16
  729.3 17.8 %multiply_convert_fusion.12 = bf16[3,512,3072]{2,1,0:T(8,128)(2,1)} fusion(f32[3,512,3072]{2,1,0:T(8,128)} %get-tuple-element.414, f32[3,512,3072]{2,1,0:T(8,128)} %fusion.166, f32[3,512]{1,0:T(4,128)S(1)} %get-tuple-element.415, f32[3,512]{1,0:T(4,128)S(1)} %dynamic-slice_bitcast_fusion.3, pred[512,3072]{1,0:T(8,128)(4,1)S(1)} %fusion.167), kind=kLoop, calls=%fused_computation.17.clone.1.clone | loop fusion | flops 28311552 | bytes 48771072 | tf_op jit(solution)/shard_map/while/body/eval_jaxpr/convert_element_type | solution.py:158
  759.8 10.8 fusion.169
  773.9 10.5 fusion.166
  786.9 14.3 multiply_reduce_fusion.16
  801.2 17.8 %multiply_convert_fusion.12 = bf16[3,512,3072]{2,1,0:T(8,128)(2,1)} fusion(f32[3,512,3072]{2,1,0:T(8,128)} %get-tuple-element.414, f32[3,512,3072]{2,1,0:T(8,128)} %fusion.166, f32[3,512]{1,0:T(4,128)S(1)} %get-tuple-element.415, f32[3,512]{1,0:T(4,128)S(1)} %dynamic-slice_bitcast_fusion.3, pred[512,3072]{1,0:T(8,128)(4,1)S(1)} %fusion.167), kind=kLoop, calls=%fused_computation.17.clone.1.clone | loop fusion | flops 28311552 | bytes 48771072 | tf_op jit(solution)/shard_map/while/body/eval_jaxpr/convert_element_type | solution.py:158
  831.6 10.8 fusion.169
  845.7 10.5 fusion.166
  858.7 14.3 multiply_reduce_fusion.16
  873.0 17.8 %multiply_convert_fusion.12 = bf16[3,512,3072]{2,1,0:T(8,128)(2,1)} fusion(f32[3,512,3072]{2,1,0:T(8,128)} %get-tuple-element.414, f32[3,512,3072]{2,1,0:T(8,128)} %fusion.166, f32[3,512]{1,0:T(4,128)S(1)} %get-tuple-element.415, f32[3,512]{1,0:T(4,128)S(1)} %dynamic-slice_bitcast_fusion.3, pred[512,3072]{1,0:T(8,128)(4,1)S(1)} %fusion.167), kind=kLoop, calls=%fused_computation.17.clone.1.clone | loop fusion | flops 28311552 | bytes 48771072 | tf_op jit(solution)/shard_map/while/body/eval_jaxpr/convert_element_type | solution.py:158
  903.5 10.8 fusion.169
  933.4 9.2 fusion.75
  942.7 10.2 fusion.86
  953.0 8.7 bitcast_convert_fusion
  961.8 8.6 add_convert_fusion.1
  970.4 21.8 %psum.69 = f32[192]{0:T(256)S(1)} all-reduce(f32[192]{0:T(256)S(1)} %copy-done.46), channel_id=1, replica_groups=mesh['dp'=8,'head'=4] {'dp'}, use_global_device_ids=true, to_apply=%region_33.34 | all-reduce | flops 192 | bytes 1536 | tf_op jit(solution)/shard_map/psum | solution.py:190
  992.8 50.2 %all-reduce.8.cloned.1.call-done = (f32[3,768,192]{1,2,0:T(8,128)}, f32[192,768]{1,0:T(8,128)}) async-done(((f32[3,768,192]{1,2,0:T(8,128)}, f32[192,768]{1,0:T(8,128)}), (f32[3,768,192]{1,2,0:T(8,128)}, f32[192,768]{1,0:T(8,128)})) %all-reduce.8.cloned.1.call-update) | async-done | bytes 2359312 | tf_op jit(solution)/shard_map/psum | solution.py:190
  1047.7 136.6 %reduce-scatter.9.cloned.1.call-done = f32[96,768]{1,0:T(8,128)} async-done(((f32[3072,768]{1,0:T(8,128)}), f32[96,768]{1,0:T(8,128)}) %reduce-scatter.9.cloned.1.call-update) | async-done | bytes 294928 | tf_op jit(solution)/shard_map/reduce_scatter | solution.py:123
  1186.1 139.4 %reduce-scatter.11.cloned.1.call-done = f32[96,768]{1,0:T(8,128)} async-done(((f32[3072,768]{1,0:T(8,128)}), f32[96,768]{1,0:T(8,128)}) %reduce-scatter.11.cloned.1.call-update) | async-done | bytes 294928 | tf_op jit(solution)/shard_map/reduce_scatter | solution.py:124
  1327.1 47.7 %reduce-scatter.7.cloned.1.call-done = bf16[768,768]{1,0:T(8,128)(2,1)} async-done(((bf16[3072,768]{1,0:T(8,128)(2,1)}), bf16[768,768]{1,0:T(8,128)(2,1)}) %reduce-scatter.7.cloned.1.call-update) | async-done | bytes 1179664 | tf_op jit(solution)/shard_map/reduce_scatter | solution.py:180
  1377.6 39.6 %all-reduce.2 = (f32[768]{0:T(1024)S(1)}, f32[768]{0:T(1024)S(1)}, f32[3072]{0:T(1024)S(1)}) all-reduce(f32[768]{0:T(1024)S(1)} %get-tuple-element.163, f32[768]{0:T(1024)S(1)} %copy-done.42, f32[3072]{0:T(1024)S(1)} %copy-done.41), channel_id=1, replica_groups=mesh['dp'=8,'head'=4] {'dp','head'}, use_global_device_ids=true, to_apply=%region_30.31 | all-reduce | flops 4608 | bytes 36864 | tf_op jit(solution)/shard_map/psum | solution.py:191
  (288 shorter events, 316.4 us)
Async XLA Ops:
  8.0 47.9 %copy-start = (bf16[3,768,192]{1,2,0:T(8,128)(2,1)S(1)}, bf16[3,768,192]{1,2,0:T(8,128)(2,1)}, u32[]{:S(2)}) copy-start(bf16[3,768,192]{1,2,0:T(8,128)(2,1)} %param.18) | copy-start | bytes 2654212
  8.0 7.6 copy-start.48
  8.0 47.8 %all-gather.5.cloned.1.call-start = ((), (), s32[]{:S(2)}) async-start(), calls=%async_computation.4 | async-start | bytes 5898240 | tf_op jit(solution)/shard_map/all_gather | solution.py:49
  8.8 51.9 %copy-start.25 = (f32[768]{0:T(1024)}, f32[768]{0:T(1024)S(1)}, u32[]{:S(2)}) copy-start(f32[768]{0:T(1024)S(1)} %convert_element_type.70) | copy-start | bytes 9220
  15.5 295.6 %reduce-scatter.5.cloned.1.call-start = ((), (), s32[]{:S(2)}) async-start(), calls=%async_computation.5 | async-start | bytes 11796480 | tf_op jit(solution)/shard_map/reduce_scatter | solution.py:81
  66.2 5.5 copy-start.3
  202.6 5.8 copy-start.10
  208.4 14.3 %copy-start.39 = (f32[192]{0:T(256)S(1)}, f32[192]{0:T(256)}, u32[]{:S(2)}) copy-start(f32[192]{0:T(256)} %convert_element_type.74) | copy-start | bytes 2308
  212.4 268.8 %copy-start.4 = (f32[24,8,6,512]{3,1,2,0:T(8,128)}, f32[24,8,6,512]{3,1,2,0:T(8,128)S(1)}, u32[]{:S(2)}) copy-start(f32[24,8,6,512]{3,1,2,0:T(8,128)S(1)} %copy.34) | copy-start | bytes 7077892
  222.8 258.4 %copy-start.18 = (f32[3072]{0:T(1024)}, f32[3072]{0:T(1024)S(1)}, u32[]{:S(2)}) copy-start(f32[3072]{0:T(1024)S(1)} %get-tuple-element.239) | copy-start | bytes 36868
  222.8 258.4 %copy-start.20 = (f32[3072]{0:T(1024)}, f32[3072]{0:T(1024)S(1)}, u32[]{:S(2)}) copy-start(f32[3072]{0:T(1024)S(1)} %get-tuple-element.240) | copy-start | bytes 36868
  228.9 82.3 %copy-start.23 = (f32[768]{0:T(1024)S(1)}, f32[768]{0:T(1024)}, u32[]{:S(2)}) copy-start(f32[768]{0:T(1024)} %copy-done.22) | copy-start | bytes 9220
  229.0 98.0 %all-gather.7.cloned.1.call-start = ((), (), s32[]{:S(2)}) async-start(), calls=%async_computation.6 | async-start | bytes 4866048 | tf_op jit(solution)/shard_map/all_gather | solution.py:89
  229.5 161.9 %all-gather.9.cloned.1.call-start = ((), (), s32[]{:S(2)}) async-start(), calls=%async_computation.7 | async-start | bytes 4866048 | tf_op jit(solution)/shard_map/all_gather | solution.py:90
  230.1 234.6 %all-gather.11.cloned.1.call-start = ((), (), s32[]{:S(2)}) async-start(), calls=%async_computation.8 | async-start | bytes 5898240 | tf_op jit(solution)/shard_map/all_gather | solution.py:127
  230.2 196.0 %copy-start.35 = (f32[768]{0:T(1024)}, f32[768]{0:T(1024)S(1)}, u32[]{:S(2)}) copy-start(f32[768]{0:T(1024)S(1)} %convert_element_type.76) | copy-start | bytes 9220
  315.1 102.1 %copy-start.43 = (f32[768]{0:T(1024)}, f32[768]{0:T(1024)S(1)}, u32[]{:S(2)}) copy-start(f32[768]{0:T(1024)S(1)} %get-tuple-element.243) | copy-start | bytes 9220
  315.1 111.2 %copy-start.37 = (f32[768]{0:T(1024)}, f32[768]{0:T(1024)S(1)}, u32[]{:S(2)}) copy-start(f32[768]{0:T(1024)S(1)} %get-tuple-element.244) | copy-start | bytes 9220
  391.5 13.0 slice-start
  391.5 13.0 slice-start.1
  391.5 13.0 slice-start.2
  404.4 12.7 copy-start.7
  417.2 9.1 copy-start.12
  417.2 9.1 copy-start.14
  428.8 614.1 %all-reduce.8.cloned.1.call-start = ((), (), s32[]{:S(2)}) async-start(), calls=%async_computation.12 | async-start | bytes 4718592 | tf_op jit(solution)/shard_map/psum | solution.py:190
  532.9 7.1 copy-start.1
  603.5 7.8 copy-start.1
  675.3 7.8 copy-start.1
  747.1 7.8 copy-start.1
  819.0 7.8 copy-start.1
  890.8 7.8 copy-start.1
  914.6 7.0 copy-start.2
  917.8 6.3 copy-start.19
  917.8 6.3 copy-start.21
  921.8 6.0 copy-start.15
  933.3 251.1 %reduce-scatter.9.cloned.1.call-start = ((), (), s32[]{:S(2)}) async-start(), calls=%async_computation.10 | async-start | bytes 9732096 | tf_op jit(solution)/shard_map/reduce_scatter | solution.py:123
  942.6 382.8 %reduce-scatter.11.cloned.1.call-start = ((), (), s32[]{:S(2)}) async-start(), calls=%async_computation.11 | async-start | bytes 9732096 | tf_op jit(solution)/shard_map/reduce_scatter | solution.py:124
  953.0 421.9 %reduce-scatter.7.cloned.1.call-start = ((), (), s32[]{:S(2)}) async-start(), calls=%async_computation.9 | async-start | bytes 5898240 | tf_op jit(solution)/shard_map/reduce_scatter | solution.py:180
  961.7 8.7 copy-start.46
  970.4 404.4 %copy-start.6 = (bf16[768,768]{1,0:T(8,128)(2,1)S(1)}, bf16[768,768]{1,0:T(8,128)(2,1)}, u32[]{:S(2)}) copy-start(bf16[768,768]{1,0:T(8,128)(2,1)} %param.15) | copy-start | bytes 3538948
  970.4 404.4 %copy-start.24 = (f32[768]{0:T(1024)S(1)}, f32[768]{0:T(1024)}, u32[]{:S(2)}) copy-start(f32[768]{0:T(1024)} %copy-done.22) | copy-start | bytes 9220
  970.4 404.4 %copy-start.26 = (f32[768]{0:T(1024)S(1)}, f32[768]{0:T(1024)}, u32[]{:S(2)}) copy-start(f32[768]{0:T(1024)} %copy-done.25) | copy-start | bytes 9220
  970.4 404.4 %copy-start.28 = (f32[768]{0:T(1024)S(1)}, f32[768]{0:T(1024)}, u32[]{:S(2)}) copy-start(f32[768]{0:T(1024)} %copy-done.27) | copy-start | bytes 9220
  970.4 404.4 %copy-start.30 = (f32[768]{0:T(1024)S(1)}, f32[768]{0:T(1024)}, u32[]{:S(2)}) copy-start(f32[768]{0:T(1024)} %copy-done.29) | copy-start | bytes 9220
  1044.9 332.7 %copy-start.41 = (f32[3072]{0:T(1024)S(1)}, f32[3072]{0:T(1024)}, u32[]{:S(2)}) copy-start(f32[3072]{0:T(1024)} %get-tuple-element.153) | copy-start | bytes 36868
  1044.9 332.7 %copy-start.42 = (f32[768]{0:T(1024)S(1)}, f32[768]{0:T(1024)}, u32[]{:S(2)}) copy-start(f32[768]{0:T(1024)} %get-tuple-element.160) | copy-start | bytes 9220
  1044.9 374.1 %copy-start.32 = (f32[768]{0:T(1024)S(1)}, f32[768]{0:T(1024)}, u32[]{:S(2)}) copy-start(f32[768]{0:T(1024)} %copy-done.31) | copy-start | bytes 9220
  1044.9 374.1 %copy-start.34 = (f32[768]{0:T(1024)S(1)}, f32[768]{0:T(1024)}, u32[]{:S(2)}) copy-start(f32[768]{0:T(1024)} %copy-done.33) | copy-start | bytes 9220
  (24 other events, 75.1 us)
Sparse Core Ops, SparseCore 0:
  15.7 40.1 all-gather.4
  229.1 82.0 reduce-scatter.4
  428.9 35.7 all-gather.10
Sparse Core Ops, SparseCore 1:
  232.4 94.5 all-gather.6
  329.7 61.7 all-gather.8
  933.4 109.5 all-reduce.7
  1048.8 135.4 reduce-scatter.8
  1190.3 135.1 reduce-scatter.10
  1328.0 46.8 reduce-scatter.6
where the time goes:
time: 1440 us; the launch traced here: 1430 us
  waiting for transfers between devices  535 us (37%)
  matrix products  484 us (34%)
  other arithmetic  219 us (15%)
  blocking collectives  124 us (9%)
  local copies, waits for them, and re-layouts  32.7 us (2%)
  loops' own time  18.6 us (1%)
  between operations  16.3 us (1%)
    reduce_scatter x1, waiting for transfers between devices, body(): lax.psum_scatter(grad_wout, ('dp', 'head'), scatter_dimension=0, tiled=True)  139 us
    reduce_scatter x1, waiting for transfers between devices, body(): lax.psum_scatter(grad_win, ('dp', 'head'), scatter_dimension=0, tiled=True)  137 us
    convert_element_type x6, other arithmetic, backward_block(): grad_logits = (probs * (grad_probs - inner)).astype(jnp.bfloat16)  107 us
    dot_general x12, matrix products, masked_scores(): jnp.einsum('qhd,khd->hqk', query_blk, keys, preferred_element_type=jnp.fl...  96.1 us
    dot_general x6, matrix products, backward_block(): jnp.einsum('qhd,khd->hqk', grad_blk, values, preferred_element_type=jnp.f...  85.7 us
    dot_general x6, matrix products, backward_block(): jnp.einsum('hqk,qhd->khd', probs.astype(jnp.bfloat16), grad_blk, preferre...  64.5 us
    dot_general x6, matrix products, forward_block(): jnp.einsum('hqk,khd->qhd', probs.astype(jnp.bfloat16), values, preferred_...  50.9 us
    psum x1, waiting for transfers between devices, body(): lax.psum((grad_wqkv, grad_wo, grad_ginner), 'dp')  50.2 us
  transfers between devices with their start and end apart: 9, of which 9 were waited for; matrix products, arithmetic and copies ran while one was open for 6% of the time, Pallas kernels for 0%

commit v1 on v0

v1 whole, which is shorter than its diff:
```python
import functools
import jax, jax.numpy as jnp
from jax import lax
from jax.experimental import pallas as pl
from jax.experimental.pallas import tpu as pltpu
HEAD_DIM=64
LONGEST=2048
NEG=-1e30
C2=0.125*1.4426950408889634
bf16=jnp.bfloat16; f32=jnp.float32
NT=(((1,),(1,)),((),()))
NN=(((1,),(0,)),((),()))
TN=(((0,),(0,)),((),()))

def dg(a,b,dims): return lax.dot_general(a,b,dims,preferred_element_type=f32)

def fwd_kernel(base_ref,q_ref,k_ref,v_ref,id_ref,o_ref,lse_ref,ks,vt,acc,ms,*,nh,bq,T,BK,tmode):
    step=pl.program_id(0)
    HD=HEAD_DIM
    @pl.when(step==0)
    def _():
        for h in range(nh):
            ks[h]=k_ref[:,h*HD:(h+1)*HD]
            vv=v_ref[:,h*HD:(h+1)*HD]
            vt[h,0:HD,:]=jnp.transpose(vv.astype(f32)).astype(bf16)
            vt[h,HD:,:]=jnp.ones((vt.shape[1]-HD,T),bf16)
    qi=base_ref[0]+step
    q=[q_ref[:,h*HD:(h+1)*HD] for h in range(nh)]
    nlong=LONGEST//bq
    in2=qi>=nlong
    def blk(k0,bk,mask,first):
        for h in range(nh):
            kb=ks[h,pl.ds(k0,bk),:]
            s=dg(kb,q[h],NT)
            if mask is not None: s=jnp.where(mask,s,NEG)
            mb=jnp.max(s,axis=0,keepdims=True)
            vb=vt[h,:,pl.ds(k0,bk)]
            if first:
                mn=mb
                p=jnp.exp2(s*C2-mn*C2)
                acc[h]=dg(vb,p.astype(bf16),NN)
            else:
                mo=ms[h]
                mn=jnp.maximum(mo,mb)
                al=jnp.exp2((mo-mn)*C2)
                p=jnp.exp2(s*C2-mn*C2)
                acc[h]=acc[h]*al+dg(vb,p.astype(bf16),NN)
            ms[h]=mn
    def idcol(k0,bk):
        r=id_ref[:,pl.ds(k0,bk)].astype(f32)
        return jnp.transpose(jnp.broadcast_to(r,(8,bk)))[:,0:1]
    q0=pl.multiple_of(qi*bq,bq)
    kr=lax.broadcasted_iota(jnp.int32,(bq,bq),0)
    qc=lax.broadcasted_iota(jnp.int32,(bq,bq),1)
    idq=id_ref[:,pl.ds(q0,bq)].astype(f32)
    @pl.when(jnp.logical_not(in2))
    def _():
        blk(q0,bq,kr<=qc,True)
        per=BK//bq
        nbig=qi//per
        def body(j,_):
            blk(pl.multiple_of(j*BK,BK),BK,None,False); return 0
        lax.fori_loop(0,nbig,body,0)
        def body2(j,_):
            blk(pl.multiple_of(j*bq,bq),bq,None,False); return 0
        lax.fori_loop(nbig*per,qi,body2,0)
    @pl.when(in2)
    def _():
        blk(q0,bq,(kr<=qc)&(idcol(q0,bq)==idq),True)
        def body(j,_):
            k0=pl.multiple_of(j*bq,bq)
            blk(k0,bq,idcol(k0,bq)==idq,False); return 0
        lax.fori_loop(nlong,qi,body,0)
    for h in range(nh):
        a=acc[h]
        l=a[HD:HD+1]
        o=a[0:HD]/l
        o_ref[:,h*HD:(h+1)*HD]=jnp.transpose(o).astype(bf16)
        lse_ref[h]=ms[h]*C2+jnp.log2(l)

def attn_fwd(base,q,k,v,ids,nq,bq=256,BK=512,tmode=0):
    T,W=k.shape; nh=W//HEAD_DIM
    full=lambda shp: pl.BlockSpec(shp,lambda i,b:tuple(0 for _ in shp))
    return pl.pallas_call(
        functools.partial(fwd_kernel,nh=nh,bq=bq,T=T,BK=BK,tmode=tmode),
        grid_spec=pltpu.PrefetchScalarGridSpec(num_scalar_prefetch=1,grid=(nq,),
            in_specs=[pl.BlockSpec((bq,W),lambda i,b:(b[0]+i,0)),full((T,W)),full((T,W)),full((1,T))],
            out_specs=[pl.BlockSpec((bq,W),lambda i,b:(i,0)),pl.BlockSpec((nh,1,bq),lambda i,b:(0,0,i))],
            scratch_shapes=[pltpu.VMEM((nh,T,HEAD_DIM),bf16),pltpu.VMEM((nh,HEAD_DIM+16,T),bf16),
                            pltpu.VMEM((nh,HEAD_DIM+16,bq),f32),pltpu.VMEM((nh,1,bq),f32)]),
        out_shape=[jax.ShapeDtypeStruct((nq*bq,W),bf16),jax.ShapeDtypeStruct((nh,1,nq*bq),f32)],
        compiler_params=pltpu.CompilerParams(dimension_semantics=("arbitrary",),vmem_limit_bytes=60*2**20),
        cost_estimate=pl.CostEstimate(flops=4*nq*bq*T//3*W,bytes_accessed=4*T*W*2,transcendentals=nq*bq*T//3*nh),
        name="attn_fwd",
    )(base,q,k,v,ids)

def bwd_kernel(base_ref,q_ref,k_ref,v_ref,id_ref,go_ref,o_ref,lse_ref,dq_ref,dk_ref,dv_ref,ks,kt,vs,dka,dva,dqa,*,nh,bq,T,BK,nq):
    step=pl.program_id(0)
    HD=HEAD_DIM
    @pl.when(step==0)
    def _():
        for h in range(nh):
            kk=k_ref[:,h*HD:(h+1)*HD]
            ks[h]=kk
            kt[h]=jnp.transpose(kk.astype(f32)).astype(bf16)
            vs[h]=v_ref[:,h*HD:(h+1)*HD]
        dka[...]=jnp.zeros_like(dka)
        dva[...]=jnp.zeros_like(dva)
    qi=base_ref[0]+step
    q=[q_ref[:,h*HD:(h+1)*HD] for h in range(nh)]
    go=[go_ref[:,h*HD:(h+1)*HD] for h in range(nh)]
    gof=go_ref[...].astype(f32)*o_ref[...].astype(f32)
    gt=jnp.transpose(gof)
    delta=[jnp.sum(gt[h*HD:(h+1)*HD],axis=0,keepdims=True) for h in range(nh)]
    lse=[lse_ref[h] for h in range(nh)]
    nlong=LONGEST//bq
    in2=qi>=nlong
    def blk(k0,bk,mask,first):
        for h in range(nh):
            kb=ks[h,pl.ds(k0,bk),:]
            vb=vs[h,pl.ds(k0,bk),:]
            s=dg(kb,q[h],NT)
            if mask is not None: s=jnp.where(mask,s,NEG)
            p=jnp.exp2(s*C2-lse[h])
            dp=dg(vb,go[h],NT)
            ds=(p*(dp-delta[h])).astype(bf16)
            dva[h,pl.ds(k0,bk),:]+=dg(p.astype(bf16),go[h],NN)
            dka[h,pl.ds(k0,bk),:]+=dg(ds,q[h],NN)
            d=dg(kt[h,:,pl.ds(k0,bk)],ds,NN)
            if first: dqa[h]=d
            else: dqa[h]+=d
    def idcol(k0,bk):
        r=id_ref[:,pl.ds(k0,bk)].astype(f32)
        return jnp.transpose(jnp.broadcast_to(r,(8,bk)))[:,0:1]
    q0=pl.multiple_of(qi*bq,bq)
    kr=lax.broadcasted_iota(jnp.int32,(bq,bq),0)
    qc=lax.broadcasted_iota(jnp.int32,(bq,bq),1)
    idq=id_ref[:,pl.ds(q0,bq)].astype(f32)
    @pl.when(jnp.logical_not(in2))
    def _():
        blk(q0,bq,kr<=qc,True)
        per=BK//bq
        nbig=qi//per
        def body(j,_):
            blk(pl.multiple_of(j*BK,BK),BK,None,False); return 0
        lax.fori_loop(0,nbig,body,0)
        def body2(j,_):
            blk(pl.multiple_of(j*bq,bq),bq,None,False); return 0
        lax.fori_loop(nbig*per,qi,body2,0)
    @pl.when(in2)
    def _():
        blk(q0,bq,(kr<=qc)&(idcol(q0,bq)==idq),True)
        def body(j,_):
            k0=pl.multiple_of(j*bq,bq)
            blk(k0,bq,idcol(k0,bq)==idq,False); return 0
        lax.fori_loop(nlong,qi,body,0)
    for h in range(nh):
        dq_ref[:,h*HD:(h+1)*HD]=(jnp.transpose(dqa[h])*0.125).astype(bf16)
    @pl.when(step==nq-1)
    def _():
        for h in range(nh):
            dk_ref[:,h*HD:(h+1)*HD]=(dka[h]*0.125).astype(bf16)
            dv_ref[:,h*HD:(h+1)*HD]=dva[h].astype(bf16)

def attn_bwd(base,q,k,v,ids,go,o,lse,nq,bq=256,BK=256):
    T,W=k.shape; nh=W//HEAD_DIM; HD=HEAD_DIM
    full=lambda shp: pl.BlockSpec(shp,lambda i,b:tuple(0 for _ in shp))
    row=lambda: pl.BlockSpec((bq,W),lambda i,b:(b[0]+i,0))
    return pl.pallas_call(
        functools.partial(bwd_kernel,nh=nh,bq=bq,T=T,BK=BK,nq=nq),
        grid_spec=pltpu.PrefetchScalarGridSpec(num_scalar_prefetch=1,grid=(nq,),
            in_specs=[row(),full((T,W)),full((T,W)),full((1,T)),row(),row(),pl.BlockSpec((nh,1,bq),lambda i,b:(0,0,b[0]+i))],
            out_specs=[pl.BlockSpec((bq,W),lambda i,b:(i,0)),full((T,W)),full((T,W))],
            scratch_shapes=[pltpu.VMEM((nh,T,HD),bf16),pltpu.VMEM((nh,HD,T),bf16),pltpu.VMEM((nh,T,HD),bf16),
                            pltpu.VMEM((nh,T,HD),f32),pltpu.VMEM((nh,T,HD),f32),pltpu.VMEM((nh,HD,bq),f32)]),
        out_shape=[jax.ShapeDtypeStruct((nq*bq,W),bf16),jax.ShapeDtypeStruct((T,W),bf16),jax.ShapeDtypeStruct((T,W),bf16)],
        compiler_params=pltpu.CompilerParams(dimension_semantics=("arbitrary",),vmem_limit_bytes=60*2**20),
        cost_estimate=pl.CostEstimate(flops=10*nq*bq*T//3*W,bytes_accessed=8*T*W*2,transcendentals=nq*bq*T//3*nh),
        name="attn_bwd",
    )(base,q,k,v,ids,go,o,lse)


from jax.sharding import PartitionSpec as P

EPSILON = 1e-05


def xor_send(value, axis, bits):
    size = lax.axis_size(axis)
    return lax.ppermute(value, axis, [(i, i ^ bits) for i in range(size)])


def rows_of(value, index, count):
    return lax.dynamic_slice_in_dim(value, index * count, count, 0)


def axis_bits(axis):
    size = lax.axis_size(axis)
    return [1 << b for b in range(size.bit_length() - 1)]


def small_sum(value, axes):
    for axis in axes:
        for bits in axis_bits(axis):
            value = value + xor_send(value, axis, bits)
    return value


def halve_sum(value, axis):
    bits = [b for b in axis_bits(axis)]
    order = [bits[0]] + bits[:0:-1]
    me = lax.axis_index(axis)
    for b in order:
        half = value.shape[0] // 2
        mine = jnp.where(me & b, 1, 0)
        got = xor_send(rows_of(value, 1 - mine, half), axis, b)
        value = (rows_of(value, mine, half).astype(f32) + got.astype(f32)).astype(value.dtype)
    for b in order[::-1]:
        got = xor_send(value, axis, b)
        value = jnp.where(
            me & b, jnp.concatenate([got, value]), jnp.concatenate([value, got])
        )
    return value


def norm_stats(values, width):
    average = jnp.sum(values, axis=-1, keepdims=True) / width
    spread = jnp.sum(values * values, axis=-1, keepdims=True) / width - average * average
    return average, lax.rsqrt(spread + EPSILON)


def norm_back(err, hat, rstd, width):
    first = jnp.sum(err, axis=-1, keepdims=True) / width
    second = jnp.sum(err * hat, axis=-1, keepdims=True) / width
    return rstd * (err - first - hat * second)


def body(layer_in, doc_ids, g_attn, w_qkv, g_inner, w_o, g_ffn, w_in, g_hidden, w_out, cotangent):
    rows, width = layer_in.shape
    group_len = doc_ids.shape[0]
    local = w_qkv.shape[2]
    parts = lax.axis_size("head")
    me = lax.axis_index("head")
    hidden = w_in.shape[0] * parts * lax.axis_size("dp")
    factor = (rows * parts * lax.axis_size("dp")) ** (-0.5)
    ga, gi, gf32 = g_attn.astype(f32), g_inner.astype(f32), g_ffn.astype(f32)
    gh32 = g_hidden.astype(f32)

    own_ids = rows_of(doc_ids, me, rows)
    valid = (own_ids >= 0).astype(f32)[:, None]
    start_x = layer_in.astype(f32) * valid
    avg_a, rstd_a = norm_stats(start_x, width)
    hat_a = (start_x - avg_a) * rstd_a
    normed = (hat_a * ga).astype(bf16)
    blocks = {0: normed}
    for b in axis_bits("head")[::-1]:
        blocks.update({k ^ b: xor_send(v, "head", b) for k, v in list(blocks.items())})
    gathered = jnp.zeros((group_len, width), bf16)
    for k, v in blocks.items():
        gathered = lax.dynamic_update_slice(gathered, v, ((me ^ k) * rows, 0))

    w_o_parts = [w_o] + [xor_send(w_o, "head", k) for k in range(1, parts)]
    gi_parts = [gi] + [xor_send(gi, "head", k) for k in range(1, parts)]
    w_out_g = (w_out.astype(f32) * gh32[:, None]).astype(bf16)
    win_full = lax.all_gather(w_in, ("dp", "head"), axis=0, tiled=True)
    wout_full = lax.all_gather(w_out_g, ("dp", "head"), axis=0, tiled=True)

    qkv = jnp.einsum("td,cde->cte", gathered, w_qkv, preferred_element_type=f32).astype(bf16)
    ids_row = doc_ids[None]
    base = jnp.zeros((1,), jnp.int32)
    bq = 512
    att, lse = attn_fwd(base, qkv[0], qkv[1], qkv[2], ids_row, group_len // bq, bq=bq, BK=1024)

    att_parts = [rows_of(att, me, rows)] + [
        xor_send(rows_of(att, me ^ k, rows), "head", k) for k in range(1, parts)
    ]
    att_parts = [v.astype(f32) for v in att_parts]
    tot = sum(jnp.sum(v, axis=-1, keepdims=True) for v in att_parts)
    tot2 = sum(jnp.sum(v * v, axis=-1, keepdims=True) for v in att_parts)
    avg_i = tot / width
    rstd_i = lax.rsqrt(tot2 / width - avg_i * avg_i + EPSILON)
    hat_i = [(v - avg_i) * rstd_i for v in att_parts]
    normed_i = [(v * g).astype(bf16) for v, g in zip(hat_i, gi_parts)]
    mixed = sum(jnp.dot(v, w, preferred_element_type=f32) for v, w in zip(normed_i, w_o_parts))
    resid = start_x + mixed

    avg_f, rstd_f = norm_stats(resid, width)
    hat_f = (resid - avg_f) * rstd_f
    ffn_in = (hat_f * gf32).astype(bf16)
    pre = lax.dot_general(ffn_in, win_full, NT, preferred_element_type=f32)
    act, act_back = jax.vjp(lambda u: jax.nn.gelu(u, approximate=False), pre)
    avg_h, rstd_h = norm_stats(act, hidden)
    hat_h = (act - avg_h) * rstd_h
    hat_h16 = hat_h.astype(bf16)
    result = (resid + jnp.dot(hat_h16, wout_full, preferred_element_type=f32)).astype(bf16)

    grad_y = cotangent.astype(f32)
    d_wout = lax.dot_general(hat_h16, cotangent, TN, preferred_element_type=f32).astype(bf16)
    err_h = lax.dot_general(cotangent, wout_full, NT, preferred_element_type=f32)
    gu = act_back(norm_back(err_h, hat_h, rstd_h, hidden))[0].astype(bf16)
    d_win = lax.dot_general(gu, ffn_in, TN, preferred_element_type=f32).astype(bf16)
    g_a = jnp.dot(gu, win_full, preferred_element_type=f32)
    part_gffn = jnp.sum(g_a * hat_f, axis=0)
    g_res = grad_y + norm_back(g_a * gf32, hat_f, rstd_f, width)
    sum_wout = lax.psum_scatter(d_wout, ("dp", "head"), scatter_dimension=0, tiled=True)
    sum_win = lax.psum_scatter(d_win, ("dp", "head"), scatter_dimension=0, tiled=True)

    gz = g_res.astype(bf16)
    d_wo = [lax.dot_general(v, gz, TN, preferred_element_type=f32) for v in normed_i]
    e_i = [
        lax.dot_general(gz, w, NT, preferred_element_type=f32) * g
        for w, g in zip(w_o_parts, gi_parts)
    ]
    first = sum(jnp.sum(e, axis=-1, keepdims=True) for e in e_i) / width
    second = sum(jnp.sum(e * v, axis=-1, keepdims=True) for e, v in zip(e_i, hat_i)) / width
    g_att = [(rstd_i * (e - first - v * second)).astype(bf16) for e, v in zip(e_i, hat_i)]
    go = jnp.zeros((group_len, local), bf16)
    for k in range(parts):
        got = xor_send(g_att[k], "head", k) if k else g_att[0]
        go = lax.dynamic_update_slice(go, got, ((me ^ k) * rows, 0))
    part_wo = d_wo[0] + sum(
        xor_send(d_wo[k].astype(bf16), "head", k).astype(f32) for k in range(1, parts)
    )
    sum_wo = halve_sum(part_wo.astype(bf16), "dp").astype(f32)

    dq, dk, dv = attn_bwd(base, qkv[0], qkv[1], qkv[2], ids_row, go, att, lse, group_len // bq, bq=bq, BK=512)

    def back_rows(k):
        return sum(
            lax.dot_general(rows_of(g, me ^ k, rows), w_qkv[c], NT, preferred_element_type=f32)
            for c, g in enumerate((dq, dk, dv))
        )

    held = {k: back_rows(k).astype(bf16) for k in reversed(range(parts))}
    for b in axis_bits("head"):
        nxt = {}
        for k in sorted(held, reverse=True):
            if k & b:
                continue
            got = xor_send(held[k ^ b], "head", b)
            nxt[k] = (held[k].astype(f32) + got.astype(f32)).astype(bf16)
        held = nxt
    g_normed = held[0].astype(f32)
    d_wqkv = jnp.stack(
        [lax.dot_general(gathered, g, TN, preferred_element_type=f32) for g in (dq, dk, dv)]
    )
    part_gattn = jnp.sum(w_qkv.astype(f32) * d_wqkv, axis=(0, 2)) / ga
    sum_wqkv = halve_sum(
        d_wqkv.astype(bf16).reshape(3 * width, local), "dp"
    ).astype(f32).reshape(3, width, local)
    small = small_sum(jnp.stack([part_gattn, part_gffn]), ("head", "dp"))

    grad_in = (g_res + norm_back(g_normed * ga, hat_a, rstd_a, width)) * valid
    sum_wout = sum_wout.astype(f32)
    return (
        result,
        grad_in,
        small[0] * factor,
        sum_wqkv * factor,
        jnp.sum(w_o.astype(f32) * sum_wo, axis=-1) / gi * factor,
        sum_wo * factor,
        small[1] * factor,
        sum_win.astype(f32) * factor,
        jnp.sum(w_out.astype(f32) * sum_wout, axis=-1) * factor,
        sum_wout * gh32[:, None] * factor,
    )


def solution(mesh):
    token, feature = P(("dp", "head"), None), P(("dp", "head"))
    weight = P(None, None, "head")
    placed = (token, P("dp"), P(), weight, P("head"), P("head", None), P(), token, feature, token, token)
    given = (token, token, P(), weight, P("head"), P("head", None), P(), token, feature, token)
    return jax.shard_map(body, mesh=mesh, in_specs=placed, out_specs=given, check_vma=False)
```

time: 1440 us -> 475 us (0.33)
  waiting for transfers between devices: 535 us -> 134 us
  matrix products: 484 us -> 112 us
  other arithmetic: 219 us -> 39.6 us
  blocking collectives: 124 us -> 0 us
  Pallas kernels: 0 us -> 66.8 us
  starting transfers between devices: 0.38 us -> 39.7 us
  local copies, waits for them, and re-layouts: 32.7 us -> 61.2 us
  loops' own time: 18.6 us -> 0 us
    dot_general x53 -> x33, matrix products: 479 us -> 108 us  [the longest x1 28.8 us: body(): pre = lax.dot_general(ffn_in, win_full, NT, preferred_element_type=f32)]
    reduce_scatter x4 -> x2, waiting for transfers between devices: 362 us -> 11.4 us  [the longest x1 11.4 us: body(): lax.psum_scatter(d_win, ('dp', 'head'), scatter_dimension=0, tiled=True)]
    ppermute x0 -> x38, waiting for transfers between devices: none -> 122 us  [xor_send(): return lax.ppermute(value, axis, [(i, i ^ bits) for i in range(size)])]
    all_gather x4 -> x2, waiting for transfers between devices: 121 us -> 0.02 us  [the longest x1 0.02 us: body(): wout_full = lax.all_gather(w_out_g, ('dp', 'head'), axis=0, tiled=True)]
    convert_element_type x16 -> x17, other arithmetic: 131 us -> 20.4 us  [the longest x1 11 us: body(): gu = act_back(norm_back(err_h, hat_h, rstd_h, hidden))[0].astype(bf16)]
    psum x4 -> x0, blocking collectives: 82 us -> none  [the longest x1 39.6 us: body(): sum_gattn, sum_gffn = lax.psum((grad_gattn, grad_gffn), ('dp', 'head'))]
    pallas_call x0 -> x2, Pallas kernels: none -> 66.8 us  [the longest x1 39.7 us: attn_bwd(): pl.pallas_call(functools.partial(bwd_kernel, nh=nh, bq=bq, T=T, BK=BK, nq...]
    psum x1 -> x0, waiting for transfers between devices: 50.2 us -> none  [body(): lax.psum((grad_wqkv, grad_wo, grad_ginner), 'dp')]
  transfers between devices with their start and end apart: 9 -> 42, of which waited for: 9 -> 18; matrix products, arithmetic and copies ran while one was open for 6% -> 32% of each run, Pallas kernels for 0% -> 14%
where the time goes in v1:
time: 475 us; the launch traced here: 469 us
  waiting for transfers between devices  134 us (28%)
  matrix products  112 us (24%)
  Pallas kernels  66.8 us (14%)
  local copies, waits for them, and re-layouts  61.2 us (13%)
  starting transfers between devices  39.7 us (8%)
  other arithmetic  39.6 us (8%)
  between operations  15.6 us (3%)
    ppermute x38, waiting for transfers between devices, xor_send(): return lax.ppermute(value, axis, [(i, i ^ bits) for i in range(size)])  122 us
    pallas_call x1, Pallas kernels, attn_bwd(): pl.pallas_call(functools.partial(bwd_kernel, nh=nh, bq=bq, T=T, BK=BK, nq...  39.7 us
    ppermute x38, starting transfers between devices, xor_send(): return lax.ppermute(value, axis, [(i, i ^ bits) for i in range(size)])  39.5 us
    dot_general x1, matrix products, body(): pre = lax.dot_general(ffn_in, win_full, NT, preferred_element_type=f32)  28.8 us
    pallas_call x1, Pallas kernels, attn_fwd(): pl.pallas_call(functools.partial(fwd_kernel, nh=nh, bq=bq, T=T, BK=BK, tm...  27.1 us
    unnamed x146, local copies, waits for them, and re-layouts  18.6 us
    reduce_scatter x1, waiting for transfers between devices, body(): lax.psum_scatter(d_win, ('dp', 'head'), scatter_dimension=0, tiled=True)  11.4 us
    dot_general x3, matrix products, body(): lax.dot_general(gathered, g, TN, preferred_element_type=f32)  11.2 us
  transfers between devices with their start and end apart: 42, of which 18 were waited for; matrix products, arithmetic and copies ran while one was open for 32% of the time, Pallas kernels for 14%

profile of v1, /device:TPU:0, one launch (start us, length us, event | category | flops | bytes accessed | tf_op | source)
XLA Modules:
  0.0 469.4 jit_solution(7365545382261717620)
XLA Ops:
  14.2 3.1 collective-permute-start
  17.3 29.2 %collective-permute-done = bf16[768,768]{0,1:T(8,128)(2,1)} collective-permute-done((bf16[768,768]{0,1:T(8,128)(2,1)S(1)}, bf16[768,768]{0,1:T(8,128)(2,1)}, u32[]{:S(2)}, u32[]{:S(2)}) %collective-permute-start) | collective-permute-done | bytes 1179680 | tf_op jit(solution)/shard_map/ppermute | solution.py:190
  47.2 2.4 broadcast_in_dim.6
  58.9 4.9 %fusion.146 = f32[3072,576]{0,1:S(1)} fusion(bf16[3072,768]{1,0:T(8,128)(2,1)} %constant_dynamic-update-slice_fusion.3, bf16[768,576]{0,1:T(8,128)(2,1)S(1)} %bitcast.101), kind=kOutput, calls=%fused_computation.260 | convolution fusion | flops 2717908992 | bytes 12681216
  63.7 2.3 convert_element_type.242
  66.1 6.3 %copy.76 = bf16[3072,3,192]{2,0,1:T(8,128)(2,1)} copy(bf16[3072,3,192]{0,2,1:T(8,128)(2,1)} %convert_element_type.242) | data formatting | bytes 7077888 | tf_op jit(solution)/shard_map/convert_element_type | solution.py:268
  72.4 4.7 %slice_bitcast_fusion = (bf16[3072,192]{1,0:T(8,128)(2,1)}, bf16[3072,192]{1,0:T(8,128)(2,1)}, bf16[3072,192]{1,0:T(8,128)(2,1)}) fusion(bf16[3,3072,192]{2,1,0:T(8,128)(2,1)} %bitcast.102), kind=kLoop, calls=%fused_computation.56 | loop fusion | bytes 7077888 | tf_op jit(solution)/shard_map/squeeze | solution.py:272
  77.1 27.1 %attn_fwd.1 = (bf16[3072,192]{1,0:T(8,128)(2,1)}, f32[3,1,3072]{2,1,0:T(1,128)}) custom-call(s32[1]{0:T(128)} %constant.59.clone.1.base_ref, bf16[3072,192]{1,0:T(8,128)(2,1)} %get-tuple-element.86.q_ref, bf16[3072,192]{1,0:T(8,128)(2,1)} %get-tuple-element.85.k_ref, bf16[3072,192]{1,0:T(8,128)(2,1)} %get-tuple-element.84.v_ref, s32[1,3072]{1,0:T(1,128)} %bitcast.110), custom_call_target="tpu_custom_call" | custom-call | flops 2415919104 | bytes 4718592 | tf_op jit(solution)/shard_map/attn_fwd/pallas_call | solution.py:84
  104.2 2.5 constant_dynamic-slice_fusion.8
  109.9 2.8 copy.78
  115.2 4.3 collective-permute-done.4
  121.4 9.2 %collective-permute-done.5 = bf16[768,192]{1,0:T(8,128)(2,1)S(1)} collective-permute-done((bf16[768,192]{1,0:T(8,128)(2,1)}, bf16[768,192]{1,0:T(8,128)(2,1)S(1)}, u32[]{:S(2)}, u32[]{:S(2)}) %collective-permute-start.5) | collective-permute-done | bytes 294944 | tf_op jit(solution)/shard_map/ppermute | solution.py:190
  130.7 2.2 collective-permute-start.10
  134.8 7.7 %collective-permute-done.9 = bf16[192,768]{1,0:T(8,128)(2,1)S(1)} collective-permute-done((bf16[192,768]{1,0:T(8,128)(2,1)}, bf16[192,768]{1,0:T(8,128)(2,1)S(1)}, u32[]{:S(2)}, u32[]{:S(2)}) %collective-permute-start.9) | collective-permute-done | bytes 294944 | tf_op jit(solution)/shard_map/ppermute | solution.py:190
  148.7 10.5 %fusion.145 = (f32[768]{0:T(1024)S(1)}, f32[3072,768]{1,0:T(8,128)}) fusion(bf16[3072,768]{1,0:T(8,128)(2,1)} %all-gather.5.cloned.1.call-done, bf16[768,768]{1,0:T(8,128)(2,1)} %param.21), kind=kOutput, calls=%fused_computation.259 | convolution fusion | flops 3626237184 | bytes 15338496 | tf_op jit(solution)/shard_map/dot_general | solution.py:299
  159.2 9.6 %copy.79 = f32[3072,768]{0,1:T(8,128)} copy(f32[3072,768]{1,0:T(8,128)} %get-tuple-element.112) | data formatting | bytes 18874368 | tf_op jit(solution)/shard_map/dot_general | solution.py:299
  168.9 28.8 %fusion.138 = (f32[768]{0:T(1024)S(1)}, f32[768]{0:T(1024)S(1)}, f32[768,3072]{1,0:T(8,128)S(1)}, f32[768,3072]{1,0:T(8,128)}) fusion(bf16[3072,768]{1,0:T(8,128)(2,1)} %all-gather.3.cloned.1.call-done, f32[768,768]{0,1:T(8,128)S(1)} %get-tuple-element.109, f32[768]{0:T(1024)S(1)} %convert_element_type.253, f32[768]{0:T(1024)S(1)} %get-tuple-element.106, ...), kind=kOutput, calls=%fused_computation.253 | convolution fusion | flops 3784309248 | bytes 25967616 | tf_op jit(solution)/shard_map/dot_general | solution.py:290
  197.7 5.4 %fusion.3 = f32[768]{0:T(1024)S(1)} fusion(f32[3072,768]{0,1:T(8,128)S(1)} %bitcast.100, f32[768]{0:T(1024)S(1)} %get-tuple-element.104, f32[768]{0:T(1024)S(1)} %get-tuple-element.103, f32[768,3072]{1,0:T(8,128)S(1)} %get-tuple-element.79, f32[768,3072]{1,0:T(8,128)} %get-tuple-element.110), kind=kLoop, calls=%fused_computation.6 | loop fusion | flops 14155008 | bytes 28320768 | tf_op jit(solution)/shard_map/reduce_sum | solution.py:234
  203.2 11.0 %add_convert_fusion = (bf16[768,3072]{1,0:T(8,128)(2,1)}, bf16[768,3072]{1,0:T(8,128)(2,1)S(1)}) fusion(f32[768,3072]{1,0:T(8,128)S(1)} %get-tuple-element.79, f32[3072,768]{0,1:T(8,128)S(1)} %bitcast.100, f32[768,3072]{1,0:T(8,128)} %get-tuple-element.110, f32[768]{0:T(1024)S(1)} %broadcast_multiply_fusion, f32[768]{0:T(1024)S(1)} %broadcast_multiply_fusion.1, ...), kind=kLoop, calls=%fused_computation.7 | loop fusion | flops 51904512 | bytes 37761024 | tf_op jit(solution)/shard_map/convert_element_type | solution.py:300
  214.1 2.2 copy-done.8
  216.3 5.6 %convolution_convert_fusion = bf16[3072,768]{1,0:T(8,128)(2,1)} fusion(bf16[768,3072]{1,0:T(8,128)(2,1)S(1)} %get-tuple-element.83, bf16[768,768]{1,0:T(8,128)(2,1)S(1)} %copy-done.27), kind=kOutput, calls=%fused_computation.25 | convolution fusion | flops 3626237952 | bytes 10616832 | tf_op jit(solution)/shard_map/dot_general | solution.py:298
  222.6 8.4 %multiply_reduce_fusion.1 = (f32[768]{0:T(1024)}, f32[768]{0:T(1024)S(1)}, f32[768]{0:T(1024)S(1)}, f32[768,768]{0,1:T(8,128)S(1)}) fusion(f32[768,768]{0,1:T(8,128)S(1)} %get-tuple-element.109, f32[768]{0:T(1024)S(1)} %copy-done.48, f32[768]{0:T(1024)S(1)} %get-tuple-element.105, f32[768]{0:T(1024)S(1)} %convert_element_type.253, ...), kind=kOutput, calls=%fused_computation.27 | convolution fusion | flops 3628594944 | bytes 14174208 | tf_op jit(solution)/shard_map/dot_general | solution.py:302
  232.4 2.2 convolution_convert_fusion.4
  235.2 2.2 convolution_convert_fusion.3
  242.2 2.9 fusion.140
  246.9 6.1 %convolution_convert_fusion.1 = bf16[3072,768]{1,0:T(8,128)(2,1)} fusion(bf16[768,3072]{1,0:T(8,128)(2,1)S(1)} %bitcast.106, f32[768,768]{0,1:T(8,128)S(1)} %get-tuple-element.109, f32[768]{0:T(1024)S(1)} %copy-done.42, f32[768]{0:T(1024)S(1)} %copy-done.49, f32[768]{0:T(1024)S(1)} %copy-done.45), kind=kOutput, calls=%fused_computation.26 | convolution fusion | flops 3628597248 | bytes 11805696 | tf_op jit(solution)/shard_map/dot_general | solution.py:301
  253.1 9.0 %add_convert_fusion.8 = bf16[768,768]{0,1:T(8,128)(2,1)} fusion(f32[768,768]{0,1:T(8,128)S(1)} %get-tuple-element.109, bf16[768,3072]{1,0:T(8,128)(2,1)} %copy-done.8, bf16[3072,768]{1,0:T(8,128)(2,1)} %all-gather.5.cloned.1.call-done), kind=kOutput, calls=%fused_computation.41 | convolution fusion | flops 3625058304 | bytes 12976128 | tf_op jit(solution)/shard_map/dot_general | solution.py:295
  266.6 2.4 copy.94
  269.7 2.5 convolution_convert_fusion.2
  274.2 5.4 %collective-permute-done.13 = bf16[768,192]{1,0:T(8,128)(2,1)} collective-permute-done((bf16[768,192]{1,0:T(8,128)(2,1)}, bf16[768,192]{1,0:T(8,128)(2,1)}, u32[]{:S(2)}, u32[]{:S(2)}) %collective-permute-start.13) | collective-permute-done | bytes 294944 | tf_op jit(solution)/shard_map/ppermute | solution.py:190
  281.4 11.6 %collective-permute-done.14 = bf16[768,192]{1,0:T(8,128)(2,1)} collective-permute-done((bf16[768,192]{1,0:T(8,128)(2,1)}, bf16[768,192]{1,0:T(8,128)(2,1)}, u32[]{:S(2)}, u32[]{:S(2)}) %collective-permute-start.14) | collective-permute-done | bytes 294944 | tf_op jit(solution)/shard_map/ppermute | solution.py:190
  294.8 39.7 %attn_bwd.1 = (bf16[3072,192]{1,0:T(8,128)(2,1)}, bf16[3072,192]{1,0:T(8,128)(2,1)}, bf16[3072,192]{1,0:T(8,128)(2,1)}) custom-call(s32[1]{0:T(128)} %constant.59.clone.1.base_ref, bf16[3072,192]{1,0:T(8,128)(2,1)} %get-tuple-element.86.q_ref, bf16[3072,192]{1,0:T(8,128)(2,1)} %get-tuple-element.85.k_ref, bf16[3072,192]{1,0:T(8,128)(2,1)} %get-tuple-element.84.v_ref, ...), custom_call_target="tpu_custom_call" | custom-call | flops 6039797760 | bytes 9437184 | tf_op jit(solution)/shard_map/attn_bwd/pallas_call | solution.py:169
  334.6 4.1 convolution_bitcast_fusion.1
  340.1 3.5 convolution_bitcast_fusion.2
  347.2 3.6 convolution_bitcast_fusion
  366.4 2.4 collective-permute-start.22
  371.6 2.5 collective-permute-start.33
  374.9 8.6 %collective-permute-done.33 = bf16[48,768]{1,0:T(8,128)(2,1)S(1)} collective-permute-done((bf16[48,768]{1,0:T(8,128)(2,1)S(1)}, bf16[48,768]{1,0:T(8,128)(2,1)S(1)}, u32[]{:S(2)}, u32[]{:S(2)}) %collective-permute-start.33) | collective-permute-done | bytes 73760 | tf_op jit(solution)/shard_map/ppermute | solution.py:190
  383.7 4.4 collective-permute-done.24
  390.5 3.2 collective-permute-done.25
  394.2 2.4 collective-permute-start.36
  396.6 10.0 %collective-permute-done.26 = bf16[288,192]{0,1:T(8,128)(2,1)S(1)} collective-permute-done((bf16[288,192]{0,1:T(8,128)(2,1)S(1)}, bf16[288,192]{0,1:T(8,128)(2,1)S(1)}, u32[]{:S(2)}, u32[]{:S(2)}) %collective-permute-start.26) | collective-permute-done | bytes 110624 | tf_op jit(solution)/shard_map/ppermute | solution.py:190
  408.2 3.7 collective-permute-start.37
  411.9 10.6 %collective-permute-done.27 = bf16[576,192]{0,1:T(8,128)(2,1)S(1)} collective-permute-done((bf16[576,192]{0,1:T(8,128)(2,1)S(1)}, bf16[576,192]{0,1:T(8,128)(2,1)S(1)}, u32[]{:S(2)}, u32[]{:S(2)}) %collective-permute-start.27) | collective-permute-done | bytes 221216 | tf_op jit(solution)/shard_map/ppermute | solution.py:190
  426.2 10.6 %collective-permute-done.28 = bf16[1152,192]{0,1:T(8,128)(2,1)S(1)} collective-permute-done((bf16[1152,192]{0,1:T(8,128)(2,1)S(1)}, bf16[1152,192]{0,1:T(8,128)(2,1)S(1)}, u32[]{:S(2)}, u32[]{:S(2)}) %collective-permute-start.28) | collective-permute-done | bytes 442400 | tf_op jit(solution)/shard_map/ppermute | solution.py:190
  440.6 3.3 add_multiply_fusion
  443.9 3.1 copy.95
  449.3 11.4 %reduce-scatter.3.cloned.1.call-done = bf16[96,768]{1,0:T(8,128)(2,1)} async-done(((bf16[3072,768]{1,0:T(8,128)(2,1)}), bf16[96,768]{1,0:T(8,128)(2,1)}) %reduce-scatter.3.cloned.1.call-update) | async-done | bytes 147472 | tf_op jit(solution)/shard_map/reduce_scatter | solution.py:306
  (307 shorter events, 92.4 us)
Async XLA Ops:
  7.2 141.5 %all-gather.5.cloned.1.call-start = ((), (), s32[]{:S(2)}) async-start(), calls=%async_computation.3 | async-start | bytes 4866048 | tf_op jit(solution)/shard_map/all_gather | solution.py:266
  10.1 158.7 %all-gather.3.cloned.1.call-start = ((), (), s32[]{:S(2)}) async-start(), calls=%async_computation.2 | async-start | bytes 4866048 | tf_op jit(solution)/shard_map/all_gather | solution.py:265
  10.8 436.1 %reduce-scatter.5.cloned.1.call-start = ((), (), s32[]{:S(2)}) async-start(), calls=%async_computation.5 | async-start | bytes 4866048 | tf_op jit(solution)/shard_map/reduce_scatter | solution.py:305
  12.5 134.9 %copy-start = (bf16[768,768]{0,1:T(8,128)(2,1)}, bf16[768,768]{0,1:T(8,128)(2,1)S(1)}, u32[]{:S(2)}) copy-start(bf16[768,768]{0,1:T(8,128)(2,1)S(1)} %copy.71) | copy-start | bytes 3538948
  12.5 34.6 %copy-start.35 = (f32[768]{0:T(1024)}, f32[768]{0:T(1024)S(1)}, u32[]{:S(2)}) copy-start(f32[768]{0:T(1024)S(1)} %convert_element_type.240) | copy-start | bytes 9220
  13.3 134.0 %copy-start.33 = (f32[768]{0:T(1024)}, f32[768]{0:T(1024)S(1)}, u32[]{:S(2)}) copy-start(f32[768]{0:T(1024)S(1)} %fusion.115) | copy-start | bytes 9220
  13.8 33.4 %copy-start.37 = (f32[768]{0:T(1024)}, f32[768]{0:T(1024)S(1)}, u32[]{:S(2)}) copy-start(f32[768]{0:T(1024)S(1)} %get-tuple-element.107) | copy-start | bytes 9220
  14.2 32.3 %collective-permute-start = (bf16[768,768]{0,1:T(8,128)(2,1)S(1)}, bf16[768,768]{0,1:T(8,128)(2,1)}, u32[]{:S(2)}, u32[]{:S(2)}) collective-permute-start(bf16[768,768]{0,1:T(8,128)(2,1)S(1)} %multiply_convert_fusion.1), channel_id=1, source_target_pairs={{0,2},{1,3},{2,0},{3,1},{4,6},{5,7},{6,4},{7,5},{8,10},{9,11},{10,... | collective-permute-start | bytes 3538952 | tf_op jit(solution)/shard_map/ppermute | solution.py:190
  17.3 35.0 %collective-permute-start.1 = (bf16[768,768]{0,1:T(8,128)(2,1)S(1)}, bf16[768,768]{0,1:T(8,128)(2,1)}, u32[]{:S(2)}, u32[]{:S(2)}) collective-permute-start(bf16[768,768]{0,1:T(8,128)(2,1)S(1)} %multiply_convert_fusion.1), channel_id=1, source_target_pairs={{0,1},{1,0},{2,3},{3,2},{4,5},{5,4},{6,7},{7,6},{8,9},{9,8},{10,11... | collective-permute-start | bytes 3538952 | tf_op jit(solution)/shard_map/ppermute | solution.py:190
  46.5 9.6 %collective-permute-start.2 = (bf16[768,768]{0,1:T(8,128)(2,1)}, bf16[768,768]{0,1:T(8,128)(2,1)}, u32[]{:S(2)}, u32[]{:S(2)}) collective-permute-start(bf16[768,768]{0,1:T(8,128)(2,1)} %collective-permute-done), channel_id=1, source_target_pairs={{0,1},{1,0},{2,3},{3,2},{4,5},{5,4},{6,7},{7,6},{8,9},{9,8},{10,11... | collective-permute-start | bytes 3538952 | tf_op jit(solution)/shard_map/ppermute | solution.py:190
  106.7 7.9 %collective-permute-start.3 = (bf16[768,192]{1,0:T(8,128)(2,1)}, bf16[768,192]{1,0:T(8,128)(2,1)S(1)}, u32[]{:S(2)}, u32[]{:S(2)}) collective-permute-start(bf16[768,192]{1,0:T(8,128)(2,1)} %get-tuple-element.87), channel_id=1, source_target_pairs={{0,1},{1,0},{2,3},{3,2},{4,5},{5,4},{6,7},{7,6},{8,9},{9,8},{10,11... | collective-permute-start | bytes 884744 | tf_op jit(solution)/shard_map/ppermute | solution.py:190
  107.2 12.2 %collective-permute-start.4 = (bf16[768,192]{1,0:T(8,128)(2,1)}, bf16[768,192]{1,0:T(8,128)(2,1)S(1)}, u32[]{:S(2)}, u32[]{:S(2)}) collective-permute-start(bf16[768,192]{1,0:T(8,128)(2,1)} %get-tuple-element.89), channel_id=1, source_target_pairs={{0,2},{1,3},{2,0},{3,1},{4,6},{5,7},{6,4},{7,5},{8,10},{9,11},{10,... | collective-permute-start | bytes 884744 | tf_op jit(solution)/shard_map/ppermute | solution.py:190
  109.5 23.7 %collective-permute-start.6 = (f32[192]{0:T(256)}, f32[192]{0:T(256)}, u32[]{:S(2)}, u32[]{:S(2)}) collective-permute-start(f32[192]{0:T(256)} %convert_element_type.248), channel_id=1, source_target_pairs={{0,1},{1,0},{2,3},{3,2},{4,5},{5,4},{6,7},{7,6},{8,9},{9,8},{10,11... | collective-permute-start | bytes 2312 | tf_op jit(solution)/shard_map/ppermute | solution.py:190
  109.5 25.3 %collective-permute-start.8 = (f32[192]{0:T(256)}, f32[192]{0:T(256)}, u32[]{:S(2)}, u32[]{:S(2)}) collective-permute-start(f32[192]{0:T(256)} %convert_element_type.248), channel_id=1, source_target_pairs={{0,2},{1,3},{2,0},{3,1},{4,6},{5,7},{6,4},{7,5},{8,10},{9,11},{10,... | collective-permute-start | bytes 2312 | tf_op jit(solution)/shard_map/ppermute | solution.py:190
  109.8 121.2 %copy-start.41 = (f32[768]{0:T(1024)}, f32[768]{0:T(1024)S(1)}, u32[]{:S(2)}) copy-start(f32[768]{0:T(1024)S(1)} %convert_element_type.253) | copy-start | bytes 9220
  112.6 18.0 %collective-permute-start.5 = (bf16[768,192]{1,0:T(8,128)(2,1)}, bf16[768,192]{1,0:T(8,128)(2,1)S(1)}, u32[]{:S(2)}, u32[]{:S(2)}) collective-permute-start(bf16[768,192]{1,0:T(8,128)(2,1)} %get-tuple-element.88), channel_id=1, source_target_pairs={{0,3},{1,2},{2,1},{3,0},{4,7},{5,6},{6,5},{7,4},{8,11},{9,10},{10,... | collective-permute-start | bytes 884744 | tf_op jit(solution)/shard_map/ppermute | solution.py:190
  114.5 18.7 %collective-permute-start.7 = (bf16[192,768]{1,0:T(8,128)(2,1)}, bf16[192,768]{1,0:T(8,128)(2,1)S(1)}, u32[]{:S(2)}, u32[]{:S(2)}) collective-permute-start(bf16[192,768]{1,0:T(8,128)(2,1)} %param.16), channel_id=1, source_target_pairs={{0,1},{1,0},{2,3},{3,2},{4,5},{5,4},{6,7},{7,6},{8,9},{9,8},{10,11... | collective-permute-start | bytes 884744 | tf_op jit(solution)/shard_map/ppermute | solution.py:190
  119.4 23.1 %collective-permute-start.9 = (bf16[192,768]{1,0:T(8,128)(2,1)}, bf16[192,768]{1,0:T(8,128)(2,1)S(1)}, u32[]{:S(2)}, u32[]{:S(2)}) collective-permute-start(bf16[192,768]{1,0:T(8,128)(2,1)} %param.16), channel_id=1, source_target_pairs={{0,2},{1,3},{2,0},{3,1},{4,6},{5,7},{6,4},{7,5},{8,10},{9,11},{10,... | collective-permute-start | bytes 884744 | tf_op jit(solution)/shard_map/ppermute | solution.py:190
  130.7 15.6 %collective-permute-start.10 = (f32[192]{0:T(256)}, f32[192]{0:T(256)S(1)}, u32[]{:S(2)}, u32[]{:S(2)}) collective-permute-start(f32[192]{0:T(256)} %convert_element_type.248), channel_id=1, source_target_pairs={{0,3},{1,2},{2,1},{3,0},{4,7},{5,6},{6,5},{7,4},{8,11},{9,10},{10,... | collective-permute-start | bytes 2312 | tf_op jit(solution)/shard_map/ppermute | solution.py:190
  133.2 14.2 %collective-permute-start.11 = (bf16[192,768]{1,0:T(8,128)(2,1)}, bf16[192,768]{1,0:T(8,128)(2,1)S(1)}, u32[]{:S(2)}, u32[]{:S(2)}) collective-permute-start(bf16[192,768]{1,0:T(8,128)(2,1)} %param.16), channel_id=1, source_target_pairs={{0,3},{1,2},{2,1},{3,0},{4,7},{5,6},{6,5},{7,4},{8,11},{9,10},{10,... | collective-permute-start | bytes 884744 | tf_op jit(solution)/shard_map/ppermute | solution.py:190
  148.7 82.3 %copy-start.44 = (f32[768]{0:T(1024)}, f32[768]{0:T(1024)S(1)}, u32[]{:S(2)}) copy-start(f32[768]{0:T(1024)S(1)} %get-tuple-element.105) | copy-start | bytes 9220
  222.0 238.8 %reduce-scatter.3.cloned.1.call-start = ((), (), s32[]{:S(2)}) async-start(), calls=%async_computation.4 | async-start | bytes 4866048 | tf_op jit(solution)/shard_map/reduce_scatter | solution.py:306
  234.6 118.4 %collective-permute-start.29 = (bf16[192,768]{1,0:T(8,128)(2,1)}, bf16[192,768]{1,0:T(8,128)(2,1)}, u32[]{:S(2)}, u32[]{:S(2)}) collective-permute-start(bf16[192,768]{1,0:T(8,128)(2,1)} %convolution_convert_fusion.4), channel_id=1, source_target_pairs={{0,1},{1,0},{2,3},{3,2},{4,5},{5,4},{6,7},{7,6},{8,9},{9,8},{10,11... | collective-permute-start | bytes 884744 | tf_op jit(solution)/shard_map/ppermute | solution.py:190
  237.4 115.7 %collective-permute-start.30 = (bf16[192,768]{1,0:T(8,128)(2,1)}, bf16[192,768]{1,0:T(8,128)(2,1)}, u32[]{:S(2)}, u32[]{:S(2)}) collective-permute-start(bf16[192,768]{1,0:T(8,128)(2,1)} %convolution_convert_fusion.3), channel_id=1, source_target_pairs={{0,2},{1,3},{2,0},{3,1},{4,6},{5,7},{6,4},{7,5},{8,10},{9,11},{10,... | collective-permute-start | bytes 884744 | tf_op jit(solution)/shard_map/ppermute | solution.py:190
  246.9 25.3 %collective-permute-start.12 = (bf16[768,192]{1,0:T(8,128)(2,1)}, bf16[768,192]{1,0:T(8,128)(2,1)}, u32[]{:S(2)}, u32[]{:S(2)}) collective-permute-start(bf16[768,192]{1,0:T(8,128)(2,1)} %get-tuple-element.95), channel_id=1, source_target_pairs={{0,1},{1,0},{2,3},{3,2},{4,5},{5,4},{6,7},{7,6},{8,9},{9,8},{10,11... | collective-permute-start | bytes 884744 | tf_op jit(solution)/shard_map/ppermute | solution.py:190
  264.8 14.8 %collective-permute-start.13 = (bf16[768,192]{1,0:T(8,128)(2,1)}, bf16[768,192]{1,0:T(8,128)(2,1)}, u32[]{:S(2)}, u32[]{:S(2)}) collective-permute-start(bf16[768,192]{1,0:T(8,128)(2,1)} %get-tuple-element.96), channel_id=1, source_target_pairs={{0,2},{1,3},{2,0},{3,1},{4,6},{5,7},{6,4},{7,5},{8,10},{9,11},{10,... | collective-permute-start | bytes 884744 | tf_op jit(solution)/shard_map/ppermute | solution.py:190
  265.1 27.9 %collective-permute-start.14 = (bf16[768,192]{1,0:T(8,128)(2,1)}, bf16[768,192]{1,0:T(8,128)(2,1)}, u32[]{:S(2)}, u32[]{:S(2)}) collective-permute-start(bf16[768,192]{1,0:T(8,128)(2,1)} %get-tuple-element.94), channel_id=1, source_target_pairs={{0,3},{1,2},{2,1},{3,0},{4,7},{5,6},{6,5},{7,4},{8,11},{9,10},{10,... | collective-permute-start | bytes 884744 | tf_op jit(solution)/shard_map/ppermute | solution.py:190
  272.2 80.9 %collective-permute-start.31 = (bf16[192,768]{1,0:T(8,128)(2,1)}, bf16[192,768]{1,0:T(8,128)(2,1)S(1)}, u32[]{:S(2)}, u32[]{:S(2)}) collective-permute-start(bf16[192,768]{1,0:T(8,128)(2,1)} %convolution_convert_fusion.2), channel_id=1, source_target_pairs={{0,3},{1,2},{2,1},{3,0},{4,7},{5,6},{6,5},{7,4},{8,11},{9,10},{10,... | collective-permute-start | bytes 884744 | tf_op jit(solution)/shard_map/ppermute | solution.py:190
  351.4 3.8 collective-permute-start.18
  355.3 3.7 collective-permute-start.19
  355.6 15.9 %collective-permute-start.32 = (bf16[96,768]{1,0:T(8,128)(2,1)S(1)}, bf16[96,768]{1,0:T(8,128)(2,1)S(1)}, u32[]{:S(2)}, u32[]{:S(2)}) collective-permute-start(bf16[96,768]{1,0:T(8,128)(2,1)S(1)} %constant_dynamic-slice_fusion.2), channel_id=1, source_target_pairs={{0,4},{4,0},{8,12},{12,8},{16,20},{20,16},{24,28},{28,24},{1,5},{5... | collective-permute-start | bytes 442376 | tf_op jit(solution)/shard_map/ppermute | solution.py:190
  359.0 3.8 collective-permute-start.20
  360.6 13.5 %collective-permute-start.23 = (bf16[1152,192]{0,1:T(8,128)(2,1)S(1)}, bf16[1152,192]{0,1:T(8,128)(2,1)S(1)}, u32[]{:S(2)}, u32[]{:S(2)}) collective-permute-start(bf16[1152,192]{0,1:T(8,128)(2,1)S(1)} %constant_dynamic-slice_fusion.5), channel_id=1, source_target_pairs={{0,4},{4,0},{8,12},{12,8},{16,20},{20,16},{24,28},{28,24},{1,5},{5... | collective-permute-start | bytes 1327112 | tf_op jit(solution)/shard_map/ppermute | solution.py:190
  362.8 3.6 collective-permute-start.21
  364.9 73.6 %collective-permute-start.15 = (bf16[768,768]{0,1:T(8,128)(2,1)S(1)}, bf16[768,768]{0,1:T(8,128)(2,1)S(1)}, u32[]{:S(2)}, u32[]{:S(2)}) collective-permute-start(bf16[768,768]{0,1:T(8,128)(2,1)S(1)} %add_convert_fusion.6), channel_id=1, source_target_pairs={{0,1},{1,0},{2,3},{3,2},{4,5},{5,4},{6,7},{7,6},{8,9},{9,8},{10,11... | collective-permute-start | bytes 3538952 | tf_op jit(solution)/shard_map/ppermute | solution.py:190
  366.4 4.5 collective-permute-start.22
  369.4 37.7 %collective-permute-start.16 = (bf16[768,768]{0,1:T(8,128)(2,1)S(1)}, bf16[768,768]{0,1:T(8,128)(2,1)S(1)}, u32[]{:S(2)}, u32[]{:S(2)}) collective-permute-start(bf16[768,768]{0,1:T(8,128)(2,1)S(1)} %add_convert_fusion.3), channel_id=1, source_target_pairs={{0,1},{1,0},{2,3},{3,2},{4,5},{5,4},{6,7},{7,6},{8,9},{9,8},{10,11... | collective-permute-start | bytes 3538952 | tf_op jit(solution)/shard_map/ppermute | solution.py:190
  371.6 11.9 %collective-permute-start.33 = (bf16[48,768]{1,0:T(8,128)(2,1)S(1)}, bf16[48,768]{1,0:T(8,128)(2,1)S(1)}, u32[]{:S(2)}, u32[]{:S(2)}) collective-permute-start(bf16[48,768]{1,0:T(8,128)(2,1)S(1)} %constant_dynamic-slice_fusion.1), channel_id=1, source_target_pairs={{0,16},{4,20},{8,24},{12,28},{16,0},{20,4},{24,8},{28,12},{1,17},{... | collective-permute-start | bytes 221192 | tf_op jit(solution)/shard_map/ppermute | solution.py:190
  374.3 13.7 %collective-permute-start.24 = (bf16[576,192]{0,1:T(8,128)(2,1)S(1)}, bf16[576,192]{0,1:T(8,128)(2,1)S(1)}, u32[]{:S(2)}, u32[]{:S(2)}) collective-permute-start(bf16[576,192]{0,1:T(8,128)(2,1)S(1)} %constant_dynamic-slice_fusion.4), channel_id=1, source_target_pairs={{0,16},{4,20},{8,24},{12,28},{16,0},{20,4},{24,8},{28,12},{1,17},{... | collective-permute-start | bytes 663560 | tf_op jit(solution)/shard_map/ppermute | solution.py:190
  383.6 4.8 %collective-permute-start.34 = (bf16[24,768]{1,0:T(8,128)(2,1)S(1)}, bf16[24,768]{1,0:T(8,128)(2,1)S(1)}, u32[]{:S(2)}, u32[]{:S(2)}) collective-permute-start(bf16[24,768]{1,0:T(8,128)(2,1)S(1)} %constant_dynamic-slice_fusion), channel_id=1, source_target_pairs={{0,8},{4,12},{8,0},{12,4},{16,24},{20,28},{24,16},{28,20},{1,9},{5... | collective-permute-start | bytes 110600 | tf_op jit(solution)/shard_map/ppermute | solution.py:190
  388.3 5.4 %collective-permute-start.25 = (bf16[288,192]{0,1:T(8,128)(2,1)S(1)}, bf16[288,192]{0,1:T(8,128)(2,1)S(1)}, u32[]{:S(2)}, u32[]{:S(2)}) collective-permute-start(bf16[288,192]{0,1:T(8,128)(2,1)S(1)} %constant_dynamic-slice_fusion.3), channel_id=1, source_target_pairs={{0,8},{4,12},{8,0},{12,4},{16,24},{20,28},{24,16},{28,20},{1,9},{5... | collective-permute-start | bytes 331784 | tf_op jit(solution)/shard_map/ppermute | solution.py:190
  388.4 5.8 %collective-permute-start.35 = (bf16[24,768]{1,0:T(8,128)(2,1)S(1)}, bf16[24,768]{1,0:T(8,128)(2,1)S(1)}, u32[]{:S(2)}, u32[]{:S(2)}) collective-permute-start(bf16[24,768]{1,0:T(8,128)(2,1)S(1)} %add_convert_fusion.15), channel_id=1, source_target_pairs={{0,8},{4,12},{8,0},{12,4},{16,24},{20,28},{24,16},{28,20},{1,9},{5... | collective-permute-start | bytes 110600 | tf_op jit(solution)/shard_map/ppermute | solution.py:190
  393.8 12.8 %collective-permute-start.26 = (bf16[288,192]{0,1:T(8,128)(2,1)S(1)}, bf16[288,192]{0,1:T(8,128)(2,1)S(1)}, u32[]{:S(2)}, u32[]{:S(2)}) collective-permute-start(bf16[288,192]{0,1:T(8,128)(2,1)S(1)} %add_convert_fusion.13), channel_id=1, source_target_pairs={{0,8},{4,12},{8,0},{12,4},{16,24},{20,28},{24,16},{28,20},{1,9},{5... | collective-permute-start | bytes 331784 | tf_op jit(solution)/shard_map/ppermute | solution.py:190
  394.2 14.0 %collective-permute-start.36 = (bf16[48,768]{1,0:T(8,128)(2,1)S(1)}, bf16[48,768]{1,0:T(8,128)(2,1)S(1)}, u32[]{:S(2)}, u32[]{:S(2)}) collective-permute-start(bf16[48,768]{1,0:T(8,128)(2,1)S(1)} %maximum_select_fusion.5), channel_id=1, source_target_pairs={{0,16},{4,20},{8,24},{12,28},{16,0},{20,4},{24,8},{28,12},{1,17},{... | collective-permute-start | bytes 221192 | tf_op jit(solution)/shard_map/ppermute | solution.py:190
  406.8 15.7 %collective-permute-start.27 = (bf16[576,192]{0,1:T(8,128)(2,1)S(1)}, bf16[576,192]{0,1:T(8,128)(2,1)S(1)}, u32[]{:S(2)}, u32[]{:S(2)}) collective-permute-start(bf16[576,192]{0,1:T(8,128)(2,1)S(1)} %maximum_select_fusion.3), channel_id=1, source_target_pairs={{0,16},{4,20},{8,24},{12,28},{16,0},{20,4},{24,8},{28,12},{1,17},{... | collective-permute-start | bytes 663560 | tf_op jit(solution)/shard_map/ppermute | solution.py:190
  408.0 30.6 %collective-permute-start.17 = (bf16[768,768]{0,1:T(8,128)(2,1)S(1)}, bf16[768,768]{0,1:T(8,128)(2,1)S(1)}, u32[]{:S(2)}, u32[]{:S(2)}) collective-permute-start(bf16[768,768]{0,1:T(8,128)(2,1)S(1)} %add_convert_fusion.2), channel_id=1, source_target_pairs={{0,2},{1,3},{2,0},{3,1},{4,6},{5,7},{6,4},{7,5},{8,10},{9,11},{10,... | collective-permute-start | bytes 3538952 | tf_op jit(solution)/shard_map/ppermute | solution.py:190
  408.2 16.5 %collective-permute-start.37 = (bf16[96,768]{1,0:T(8,128)(2,1)S(1)}, bf16[96,768]{1,0:T(8,128)(2,1)S(1)}, u32[]{:S(2)}, u32[]{:S(2)}) collective-permute-start(bf16[96,768]{1,0:T(8,128)(2,1)S(1)} %maximum_select_fusion.4), channel_id=1, source_target_pairs={{0,4},{4,0},{8,12},{12,8},{16,20},{20,16},{24,28},{28,24},{1,5},{5... | collective-permute-start | bytes 442376 | tf_op jit(solution)/shard_map/ppermute | solution.py:190
  422.8 14.0 %collective-permute-start.28 = (bf16[1152,192]{0,1:T(8,128)(2,1)S(1)}, bf16[1152,192]{0,1:T(8,128)(2,1)S(1)}, u32[]{:S(2)}, u32[]{:S(2)}) collective-permute-start(bf16[1152,192]{0,1:T(8,128)(2,1)S(1)} %maximum_select_fusion.1), channel_id=1, source_target_pairs={{0,4},{4,0},{8,12},{12,8},{16,20},{20,16},{24,28},{28,24},{1,5},{5... | collective-permute-start | bytes 1327112 | tf_op jit(solution)/shard_map/ppermute | solution.py:190
  (65 other events, 444.9 us)
Sparse Core Ops, SparseCore 0:
  10.9 67.6 all-gather.4
  81.5 70.0 all-gather.2
  222.1 117.2 reduce-scatter.4
  344.7 115.9 reduce-scatter.2
